TPU v7x, 32 devices: a whole 2x2x4 slice. The times are simulated.
32 devices in a mesh: narrow: 4 (over y, x), region: 8 (over z, core).
Axes of the slice: x: 2, y: 2, z: 4, core: 2. Of those that a mesh axis runs over, the one named last changes fastest.
Arguments:
- point_feats: bfloat16 [64, 131072], P(None, ('narrow', 'region')), may hold values from -6 to 6
- point_owner: int32 [131072, 1], P(('narrow', 'region')), may hold values from 0 to 31; in each aligned block of 4096 rows (0 to 4095, 4096 to 8191, ...) at most 256 rows name the same one
- point_voxel: int32 [131072], P(('narrow', 'region')), may hold values from 0 to 12287
- weight: bfloat16 [9, 64, 192], replicated, may hold values from -0.15625 to 0.15625
- cotangent: bfloat16 [64, 192, 2048], P(None, 'region', 'narrow'), may hold values from -6 to 6
Outputs:
- conv_out: bfloat16 [64, 192, 2048], P(None, 'region', 'narrow')
- point_grad: bfloat16 [64, 131072], P(None, ('narrow', 'region'))
- weight_grad: float32 [9, 64, 192], replicated
Inputs may be any that keep to these rules, and one draw needn't show every extreme that they name: `point_owner`: among the 4096 points of one device no owner is named more than 256 times, a bound that some block reaches.
All inputs are finite; a program needn't handle non-finite values.
Results may differ from a plain program's by a relative error of at most 0.0036.
Values may be sent and summed in bfloat16 or wider, within the bound.
A program may use at most 192 MiB of HBM per device.

v0:
```python
import math
import jax
import jax.numpy as jnp
from jax import lax
from jax.sharding import PartitionSpec as P

NZ = 64
CY = 8


def extended(cells, sides, width):
    for axis, dim in sides:
        count = lax.axis_size(axis)
        ends = count - 1
        head = lax.slice_in_dim(cells, 0, width, axis=dim)
        tail = lax.slice_in_dim(cells, cells.shape[dim] - width, cells.shape[dim], axis=dim)
        cells = jnp.concatenate(
            [
                lax.ppermute(tail, axis, [(i, (i + 1) % count) for i in range(ends)]),
                cells,
                lax.ppermute(head, axis, [((i + 1) % count, i) for i in range(ends)]),
            ],
            axis=dim,
        )
    return cells


def stack_depth(padded, offsets, depth):
    return jnp.concatenate([padded[..., o : o + depth] for o in offsets], axis=0)


def shards(point_feats, point_owner, point_voxel, weight, cotangent):
    n_narrow = lax.axis_size("narrow")
    n_region = lax.axis_size("region")
    devices = n_narrow * n_region
    chans, points_here = point_feats.shape
    slots = 2 * points_here // devices
    rows_x = cotangent.shape[1]
    voxels = rows_x * CY * NZ
    owner = point_owner[:, 0]
    marks = (owner[:, None] == jnp.arange(devices, dtype=jnp.int32)[None, :]).astype(jnp.int32)
    slot = jnp.sum(jnp.cumsum(marks, axis=0) * marks, axis=1) - 1
    send_feats = jnp.zeros((devices, slots, chans), jnp.bfloat16).at[owner, slot].set(point_feats.T)
    send_feats = send_feats.reshape(devices, slots * chans)
    send_vox = jnp.zeros((devices, slots), jnp.int32).at[owner, slot].set(point_voxel)
    got_feats, got_vox = (
        lax.all_to_all(send_feats, ("narrow", "region"), split_axis=0, concat_axis=0, tiled=True),
        lax.all_to_all(send_vox, ("narrow", "region"), split_axis=0, concat_axis=0, tiled=True),
    )
    incoming = got_feats.reshape(devices * slots, chans).astype(jnp.float32)
    targets = got_vox.reshape(devices * slots)
    sums = jax.ops.segment_sum(incoming, targets, num_segments=voxels)
    grid = sums.T.astype(jnp.bfloat16).reshape(chans, rows_x, CY, NZ)
    grads = cotangent.reshape(chans, rows_x, CY, NZ)
    padded = extended(grid, (("narrow", 2), ("region", 1)), 1)
    gpad = extended(grads, (("narrow", 2), ("region", 1)), 1)
    padded = jnp.pad(padded, ((0, 0), (0, 0), (0, 0), (1, 1)))
    stacked = stack_depth(padded, [0, 1, 2], NZ)
    gpad = jnp.pad(gpad, ((0, 0), (0, 0), (0, 0), (1, 1)))
    gstack = stack_depth(gpad, [2, 1, 0], NZ)
    flipped = weight.reshape(9, chans, 3, chans).transpose(0, 3, 2, 1).reshape(9, chans, 3 * chans)
    result = jnp.zeros((chans, rows_x, CY, NZ), jnp.float32)
    backward = jnp.zeros((chans, rows_x, CY, NZ), jnp.float32)
    kernels = []
    for a in range(3):
        for b in range(3):
            k = a * 3 + b
            window = stacked[:, a : a + rows_x, b : b + CY]
            result = result + jnp.einsum(
                "ok,kxyz->oxyz", weight[k], window, preferred_element_type=jnp.float32
            )
            kernels.append(
                jnp.einsum("oxyz,kxyz->ok", grads, window, preferred_element_type=jnp.float32)
            )
            backward = backward + jnp.einsum(
                "ck,kxyz->cxyz",
                flipped[k],
                gstack[:, 2 - a : 2 - a + rows_x, 2 - b : 2 - b + CY],
                preferred_element_type=jnp.float32,
            )
    conv_out = result.astype(jnp.bfloat16).reshape(chans, rows_x, CY * NZ)
    total_cells = rows_x * n_region * CY * n_narrow * NZ
    weight_grad = lax.psum(jnp.stack(kernels), ("narrow", "region")) * (
        1.0 / math.sqrt(total_cells)
    )
    grad_flat = backward.astype(jnp.bfloat16).reshape(chans, voxels)
    picked = jnp.take(grad_flat, targets, axis=1).T.reshape(devices, slots * chans)
    returned = lax.all_to_all(picked, ("narrow", "region"), split_axis=0, concat_axis=0, tiled=True)
    returned = returned.reshape(devices, slots, chans)
    point_grad = returned[owner, slot].T
    return (conv_out, point_grad, weight_grad)


def solution(mesh):
    in_specs = (
        P(None, ("narrow", "region")),
        P(("narrow", "region"), None),
        P(("narrow", "region")),
        P(),
        P(None, "region", "narrow"),
    )
    out_specs = (P(None, "region", "narrow"), P(None, ("narrow", "region")), P())
    return jax.shard_map(shards, mesh=mesh, in_specs=in_specs, out_specs=out_specs, check_vma=False)
```

profile of v0, /device:TPU:0, one launch (start us, length us, event | category | flops | bytes accessed | tf_op | source)
XLA Modules:
  0.0 687.5 jit_solution(5900122822803206030)
XLA Ops:
  7.9 9.2 %reduce-window.6 = s32[32,32,128]{2,1,0:T(8,128)S(1)} reduce-window(s32[32,32,128]{2,1,0:T(8,128)S(1)} %fusion.21, s32[]{:T(128)} %constant.14.clone.1), window={size=1x1x128 pad=0_0x0_0x127_0}, to_apply=%region_0.0 | reduce-window | flops 16646144 | bytes 1048580 | tf_op jit(solution)/shard_map/reduce-window
  21.8 16.3 %scatter_custom_fusion.1 = s32[8192]{0:T(1024)} fusion(s32[4096]{0:T(1024)S(1)} %broadcast_select_fusion.1, s32[4096]{0:T(1024)} %param.7, s32[]{:T(128)} %constant.14.clone.1), kind=kCustom, calls=%fused_computation.98 | custom fusion | bytes 33280
  38.1 7.4 %all-to-all-start = ((s32[32,1,256]{2,1,0:T(1,128)}), s32[32,1,256]{2,1,0:T(1,128)}, u32[]{:S(2)}, u32[]{:S(2)}) async-start(s32[32,1,256]{2,1,0:T(1,128)} %bitcast.5), calls=%async_computation | async-start | bytes 65536 | tf_op jit(solution)/shard_map/all_to_all | solution.py:48
  60.9 12.9 %scatter_custom_fusion.2 = bf16[8192,64]{1,0:T(8,128)(2,1)} fusion(s32[4096]{0:T(1024)} %copy-done.17, bf16[4096,64]{1,0:T(8,128)(2,1)} %copy.54, bf16[]{:T(256)} %constant.33.clone.1), kind=kCustom, calls=%fused_computation.45 | custom fusion | bytes 1049088
  73.8 6.2 all_to_all.24
  80.6 9.4 %reduce.11 = bf16[32,16384]{1,0:T(8,128)(2,1)} reduce(bf16[32,1,16384]{2,1,0:T(2,128)(2,1)} %all_to_all.24, bf16[]{:T(256)} %broadcast.231), dimensions={1}, to_apply=%all_to_all.24.reduce_sub_computation | reduce | bytes 2097154 | tf_op jit(solution)/shard_map/all_to_all | solution.py:47
  106.1 7.6 %all-to-all-start.1 = ((bf16[32,2,8192]{2,1,0:T(2,128)(2,1)}), bf16[32,2,8192]{2,1,0:T(2,128)(2,1)}, u32[]{:S(2)}, u32[]{:S(2)}) async-start(bf16[32,2,8192]{2,1,0:T(2,128)(2,1)} %reshape.224), calls=%async_computation.1 | async-start | bytes 2097152 | tf_op jit(solution)/shard_map/all_to_all | solution.py:47
  122.4 9.0 %select_maximum_fusion = bf16[64,26,10,66]{0,3,2,1:T(8,128)(2,1)S(1)} fusion(bf16[64,1,10,64]{0,3,2,1:T(8,128)(2,1)S(1)} %collective-permute-done.7, bf16[64,1,10,64]{0,3,2,1:T(8,128)(2,1)S(1)} %collective-permute-done.6, bf16[64,24,1,64]{0,3,2,1:T(8,128)(2,1)} %collective-permute-done.5, bf16[64,24,8,64]{0,3,2,1:T(8,128)(2,1)S(1)} %bitcast.265, ...), kind=kLoop, calls=%fused_computation.12 | loop fusion | flops 19768320 | bytes 4326400 | tf_op jit(solution)/shard_map/concatenate | solution.py:17
  133.8 11.6 %pad_maximum_fusion.1 = bf16[192,26,10,64]{0,3,2,1:T(8,128)(2,1)S(1)} fusion(bf16[64,26,10,64]{0,3,2,1:T(8,128)(2,1)S(1)} %get-tuple-element.15, bf16[64,1,10,64]{0,3,2,1:T(8,128)(2,1)S(1)} %collective-permute-done.7, bf16[64,24,1,64]{0,3,2,1:T(8,128)(2,1)} %collective-permute-done.5, bf16[64,24,8,64]{0,3,2,1:T(8,128)(2,1)S(1)} %bitcast.266, ...), kind=kLoop, calls=%fused_computation.9 | loop fusion | flops 44728320 | bytes 12779520 | tf_op jit(solution)/shard_map/concatenate | solution.py:29
  181.2 18.4 %add_convert_fusion = bf16[24,8,64,64]{3,2,1,0:T(8,128)(2,1)} fusion(f32[24,8,64,64]{3,2,1,0:T(8,128)} %fusion.62, f32[24,8,64,64]{3,2,1,0:T(8,128)} %fusion.61, f32[24,8,64,64]{3,2,1,0:T(8,128)} %fusion.60, f32[24,8,64,64]{3,2,1,0:T(8,128)} %fusion.59, f32[24,8,64,64]{3,2,1,0:T(8,128)} %fusion.58, f32[24,8,64,64]{3,2,1,0:T(8,128)} %fusion.57, ...), kind=kOutput, calls=%fused_computation.10 | convolution fusion | flops 309067776 | bytes 33153024 | tf_op jit(solution)/shard_map/ck,kxyz->cxyz/dot_general | solution.py:75
  199.6 30.4 %gather_fusion = bf16[8192,64]{1,0:T(8,128)(2,1)} fusion(bf16[64,12288]{0,1:T(8,128)(2,1)} %bitcast.281, s32[8192]{0:T(1024)S(1)} %copy-done.15), kind=kCustom, calls=%fused_computation | custom fusion | bytes 2129920 | tf_op jit(solution)/shard_map/jit(_take)/gather | solution.py:87
  230.1 6.6 broadcast_select_fusion
  236.6 6.2 all_to_all.25
  242.8 9.4 %reduce.12 = bf16[32,16384]{1,0:T(8,128)(2,1)} reduce(bf16[32,1,16384]{2,1,0:T(2,128)(2,1)} %all_to_all.25, bf16[]{:T(256)} %broadcast.231), dimensions={1}, to_apply=%all_to_all.25.reduce_sub_computation | reduce | bytes 2097154 | tf_op jit(solution)/shard_map/all_to_all | solution.py:88
  254.8 21.9 %all-to-all-start.2 = ((bf16[32,2,8192]{2,1,0:T(2,128)(2,1)}), bf16[32,2,8192]{2,1,0:T(2,128)(2,1)}, u32[]{:S(2)}, u32[]{:S(2)}) async-start(bf16[32,2,8192]{2,1,0:T(2,128)(2,1)} %reshape.226), calls=%async_computation.2 | async-start | bytes 2097152 | tf_op jit(solution)/shard_map/all_to_all | solution.py:88
  282.7 9.0 %convert_reduce_fusion = f32[32,16384]{1,0:T(8,128)} fusion(bf16[32,1,16384]{2,1,0:T(2,128)(2,1)} %reshape.225), kind=kLoop, calls=%fused_computation.25 | loop fusion | flops 524288 | bytes 3145728 | tf_op jit(solution)/shard_map/convert_element_type | solution.py:50
  296.0 52.3 %scatter_custom_fusion = f32[12288,64]{1,0:T(8,128)} fusion(s32[8192]{0:T(1024)} %bitcast.6, f32[8192,64]{1,0:T(8,128)} %reshape.171, f32[]{:T(128)} %constant.13.clone.1), kind=kCustom, calls=%fused_computation.23 | custom fusion | flops 524288 | bytes 3146240 | tf_op jit(solution)/shard_map/scatter-add | solution.py:52
  351.4 8.3 %collective-permute-start = (bf16[64,24,1,64]{0,3,2,1:T(8,128)(2,1)S(1)}, bf16[64,24,1,64]{0,3,2,1:T(8,128)(2,1)S(1)}, u32[]{:S(2)}, u32[]{:S(2)}) collective-permute-start(bf16[64,24,1,64]{0,3,2,1:T(8,128)(2,1)S(1)} %get-tuple-element.24), channel_id=1, source_target_pairs={{0,8},{8,16},{16,24},{1,9},{9,17},{17,25},{2,10},{10,18},{18,26},{... | collective-permute-start | bytes 589832 | tf_op jit(solution)/shard_map/ppermute | solution.py:19
  381.3 8.7 %reduce.6 = bf16[32,16384]{1,0:T(8,128)(2,1)} reduce(bf16[32,1,16384]{2,1,0:T(2,128)(2,1)} %reshape.227, bf16[]{:T(256)} %constant.72), dimensions={1}, to_apply=%all_to_all.23.reduce_sub_computation | reduce | bytes 2097154 | tf_op jit(solution)/shard_map/all_to_all | solution.py:88
  394.0 67.6 %gather_fusion.1 = bf16[4096,64]{1,0:T(8,128)(2,1)} fusion(bf16[32,256,64]{2,1,0:T(8,128)(2,1)} %reshape.141, s32[4096]{0:T(1024)S(1)} %bitcast.276), kind=kCustom, calls=%fused_computation.1 | custom fusion | bytes 1081344 | tf_op jit(solution)/shard_map/gather | solution.py:90
  464.0 9.6 %select_maximum_fusion.4 = bf16[64,26,10,66]{0,3,2,1:T(8,128)(2,1)S(1)} fusion(bf16[64,1,10,64]{0,3,2,1:T(8,128)(2,1)} %collective-permute-done.3, bf16[64,1,10,64]{0,3,2,1:T(8,128)(2,1)} %collective-permute-done.2, bf16[64,24,1,64]{0,3,2,1:T(8,128)(2,1)} %copy-done.3, bf16[64,24,8,64]{0,3,2,1:T(8,128)(2,1)} %bitcast.279, ...), kind=kLoop, calls=%fused_computation.16 | loop fusion | flops 19768320 | bytes 4326400 | tf_op jit(solution)/shard_map/concatenate | solution.py:17
  475.9 11.3 %pad_maximum_fusion = bf16[192,26,10,64]{0,3,2,1:T(8,128)(2,1)S(1)} fusion(bf16[64,26,10,64]{0,3,2,1:T(8,128)(2,1)S(1)} %get-tuple-element.17, bf16[64,1,10,64]{0,3,2,1:T(8,128)(2,1)} %collective-permute-done.3, bf16[64,24,1,64]{0,3,2,1:T(8,128)(2,1)S(1)} %copy-done.4, bf16[64,24,8,64]{0,3,2,1:T(8,128)(2,1)S(1)} %bitcast.280, ...), kind=kLoop, calls=%fused_computation.8 | loop fusion | flops 44728320 | bytes 12779520 | tf_op jit(solution)/shard_map/concatenate | solution.py:29
  542.3 18.5 %add_convert_fusion.1 = bf16[24,8,64,64]{3,2,1,0:T(8,128)(2,1)S(1)} fusion(f32[24,8,64,64]{3,2,1,0:T(8,128)} %fusion.23, f32[24,8,64,64]{3,2,1,0:T(8,128)} %fusion.25, f32[24,8,64,64]{3,2,1,0:T(8,128)} %fusion.27, f32[24,8,64,64]{3,2,1,0:T(8,128)} %fusion.29, f32[24,8,64,64]{3,2,1,0:T(8,128)} %fusion.31, f32[24,8,64,64]{3,2,1,0:T(8,128)} %fusion.33, ...), kind=kOutput, calls=%fused_computation.11 | convolution fusion | flops 309067776 | bytes 33161216 | tf_op jit(solution)/shard_map/ok,kxyz->oxyz/dot_general | solution.py:69
  564.0 114.5 %all-reduce.4.cloned.1.call-done = f32[9,64,192]{2,1,0:T(8,128)} async-done(((f32[9,64,192]{2,1,0:T(8,128)}), f32[9,64,192]{2,1,0:T(8,128)}) %all-reduce.4.cloned.1.call-update) | async-done | bytes 442384 | tf_op jit(solution)/shard_map/psum | solution.py:83
  (124 shorter events, 190.6 us)
Async XLA Ops:
  21.8 16.3 %copy-start.17 = (s32[4096]{0:T(1024)}, s32[4096]{0:T(1024)S(1)}, u32[]{:S(2)}) copy-start(s32[4096]{0:T(1024)S(1)} %broadcast_select_fusion.1) | copy-start | bytes 49156
  38.1 68.0 %all-to-all-start = ((s32[32,1,256]{2,1,0:T(1,128)}), s32[32,1,256]{2,1,0:T(1,128)}, u32[]{:S(2)}, u32[]{:S(2)}) async-start(s32[32,1,256]{2,1,0:T(1,128)} %bitcast.5), calls=%async_computation | async-start | bytes 65536 | tf_op jit(solution)/shard_map/all_to_all | solution.py:48
  49.9 65.2 %collective-permute-start.4 = (bf16[64,24,1,64]{0,3,2,1:T(8,128)(2,1)}, bf16[64,24,1,64]{0,3,2,1:T(8,128)(2,1)S(1)}, u32[]{:S(2)}, u32[]{:S(2)}) collective-permute-start(bf16[64,24,1,64]{0,3,2,1:T(8,128)(2,1)} %get-tuple-element.22), channel_id=1, source_target_pairs={{0,8},{8,16},{16,24},{1,9},{9,17},{17,25},{2,10},{10,18},{18,26},{... | collective-permute-start | bytes 589832 | tf_op jit(solution)/shard_map/ppermute | solution.py:19
  53.5 61.6 %collective-permute-start.5 = (bf16[64,24,1,64]{0,3,2,1:T(8,128)(2,1)}, bf16[64,24,1,64]{0,3,2,1:T(8,128)(2,1)}, u32[]{:S(2)}, u32[]{:S(2)}) collective-permute-start(bf16[64,24,1,64]{0,3,2,1:T(8,128)(2,1)} %get-tuple-element.23), channel_id=1, source_target_pairs={{8,0},{16,8},{24,16},{9,1},{17,9},{25,17},{10,2},{18,10},{26,18},{... | collective-permute-start | bytes 589832 | tf_op jit(solution)/shard_map/ppermute | solution.py:21
  106.1 148.8 %all-to-all-start.1 = ((bf16[32,2,8192]{2,1,0:T(2,128)(2,1)}), bf16[32,2,8192]{2,1,0:T(2,128)(2,1)}, u32[]{:S(2)}, u32[]{:S(2)}) async-start(bf16[32,2,8192]{2,1,0:T(2,128)(2,1)} %reshape.224), calls=%async_computation.1 | async-start | bytes 2097152 | tf_op jit(solution)/shard_map/all_to_all | solution.py:47
  115.9 4.8 collective-permute-start.6
  118.0 4.4 collective-permute-start.7
  133.7 11.6 %copy-start.7 = (bf16[1,64,3,64]{1,3,2,0:T(8,128)(2,1)S(1)}, bf16[1,64,3,64]{1,3,2,0:T(8,128)(2,1)}, u32[]{:S(2)}) copy-start(bf16[1,64,3,64]{1,3,2,0:T(8,128)(2,1)} %copy.58) | copy-start | bytes 73732
  145.4 4.5 copy-start.8
  149.8 4.4 copy-start.9
  158.6 4.4 copy-start.11
  163.0 4.5 copy-start.12
  171.9 4.4 copy-start.14
  176.3 4.9 copy-start.6
  181.2 18.4 %copy-start.15 = (s32[8192]{0:T(1024)S(1)}, s32[8192]{0:T(1024)}, u32[]{:S(2)}) copy-start(s32[8192]{0:T(1024)} %broadcast_clamp_fusion) | copy-start | bytes 98308
  199.6 30.4 %copy-start.16 = (pred[8192]{0:T(1024)(128)(4,1)S(1)}, pred[8192]{0:T(1024)(128)(4,1)}, u32[]{:S(2)}) copy-start(pred[8192]{0:T(1024)(128)(4,1)} %compare_and_fusion) | copy-start | bytes 24580
  254.8 120.2 %all-to-all-start.2 = ((bf16[32,2,8192]{2,1,0:T(2,128)(2,1)}), bf16[32,2,8192]{2,1,0:T(2,128)(2,1)}, u32[]{:S(2)}, u32[]{:S(2)}) async-start(bf16[32,2,8192]{2,1,0:T(2,128)(2,1)} %reshape.226), calls=%async_computation.2 | async-start | bytes 2097152 | tf_op jit(solution)/shard_map/all_to_all | solution.py:88
  276.8 401.7 %all-reduce.4.cloned.1.call-start = ((), (), s32[]{:S(2)}) async-start(), calls=%async_computation.3 | async-start | bytes 1179648 | tf_op jit(solution)/shard_map/psum | solution.py:83
  351.4 19.6 %copy-start.1 = (bf16[12288,64]{1,0:T(8,128)(2,1)}, bf16[12288,64]{1,0:T(8,128)(2,1)S(1)}, u32[]{:S(2)}) copy-start(bf16[12288,64]{1,0:T(8,128)(2,1)S(1)} %convert_element_type.29) | copy-start | bytes 4718596
  351.4 13.6 %collective-permute-start = (bf16[64,24,1,64]{0,3,2,1:T(8,128)(2,1)S(1)}, bf16[64,24,1,64]{0,3,2,1:T(8,128)(2,1)S(1)}, u32[]{:S(2)}, u32[]{:S(2)}) collective-permute-start(bf16[64,24,1,64]{0,3,2,1:T(8,128)(2,1)S(1)} %get-tuple-element.24), channel_id=1, source_target_pairs={{0,8},{8,16},{16,24},{1,9},{9,17},{17,25},{2,10},{10,18},{18,26},{... | collective-permute-start | bytes 589832 | tf_op jit(solution)/shard_map/ppermute | solution.py:19
  359.8 11.2 %collective-permute-start.1 = (bf16[64,24,1,64]{0,3,2,1:T(8,128)(2,1)S(1)}, bf16[64,24,1,64]{0,3,2,1:T(8,128)(2,1)S(1)}, u32[]{:S(2)}, u32[]{:S(2)}) collective-permute-start(bf16[64,24,1,64]{0,3,2,1:T(8,128)(2,1)S(1)} %get-tuple-element.25), channel_id=1, source_target_pairs={{8,0},{16,8},{24,16},{9,1},{17,9},{25,17},{10,2},{18,10},{26,18},{... | collective-permute-start | bytes 589832 | tf_op jit(solution)/shard_map/ppermute | solution.py:21
  371.8 92.2 %collective-permute-start.2 = (bf16[64,1,10,64]{0,3,2,1:T(8,128)(2,1)}, bf16[64,1,10,64]{0,3,2,1:T(8,128)(2,1)}, u32[]{:S(2)}, u32[]{:S(2)}) collective-permute-start(bf16[64,1,10,64]{0,3,2,1:T(8,128)(2,1)} %get-tuple-element.20), channel_id=1, source_target_pairs={{0,1},{1,2},{2,3},{3,4},{4,5},{5,6},{6,7},{8,9},{9,10},{10,11},{11... | collective-permute-start | bytes 245768 | tf_op jit(solution)/shard_map/ppermute | solution.py:19
  373.8 90.2 %collective-permute-start.3 = (bf16[64,1,10,64]{0,3,2,1:T(8,128)(2,1)}, bf16[64,1,10,64]{0,3,2,1:T(8,128)(2,1)}, u32[]{:S(2)}, u32[]{:S(2)}) collective-permute-start(bf16[64,1,10,64]{0,3,2,1:T(8,128)(2,1)} %get-tuple-element.21), channel_id=1, source_target_pairs={{1,0},{2,1},{3,2},{4,3},{5,4},{6,5},{7,6},{9,8},{10,9},{11,10},{12... | collective-permute-start | bytes 245768 | tf_op jit(solution)/shard_map/ppermute | solution.py:21
  487.2 53.0 %copy-start = (bf16[192,26,10,64]{0,3,2,1:T(8,128)(2,1)}, bf16[192,26,10,64]{0,3,2,1:T(8,128)(2,1)S(1)}, u32[]{:S(2)}) copy-start(bf16[192,26,10,64]{0,3,2,1:T(8,128)(2,1)S(1)} %pad_maximum_fusion) | copy-start | bytes 19169284
  (6 other events, 17.1 us)
Sparse Core Ops, SparseCore 0:
  542.4 135.9 all-reduce.3
where the time goes:
time: 696 us; the launch traced here: 687 us
  local copies, waits for them, and re-layouts  201 us (29%)
  other arithmetic  160 us (23%)
  matrix products  128 us (18%)
  waiting for transfers between devices  126 us (18%)
  starting transfers between devices  58.1 us (8%)
  between operations  14.6 us (2%)
    psum x1, waiting for transfers between devices, shards(): lax.psum(jnp.stack(kernels), ('narrow', 'region'))  114 us
    gather x1, local copies, waits for them, and re-layouts, shards(): point_grad = returned[owner, slot].T  67.6 us
    unnamed x46, local copies, waits for them, and re-layouts  57.5 us
    dot_general x9, matrix products, shards(): jnp.einsum('ck,kxyz->cxyz', flipped[k], gstack[:, 2 - a:2 - a + rows_x, 2...  54.2 us
    dot_general x9, matrix products, shards(): jnp.einsum('ok,kxyz->oxyz', weight[k], window, preferred_element_type=jnp...  53.8 us
    scatter-add x1, other arithmetic, shards(): sums = jax.ops.segment_sum(incoming, targets, num_segments=voxels)  52.3 us
    gather x1, local copies, waits for them, and re-layouts, shards(): jnp.take(grad_flat, targets, axis=1).T.reshape(devices, slots * chans)  30.4 us
    concatenate x2, other arithmetic, stack_depth(): return jnp.concatenate([padded[..., o:o + depth] for o in offsets], axis=0)  22.9 us
  transfers between devices with their start and end apart: 12, of which 4 were waited for; matrix products, arithmetic and copies ran while one was open for 53% of the time, Pallas kernels for 0%

commit v1 on v0

--- a/solution.py
+++ b/solution.py
@@ -6,6 +6,11 @@
 
 NZ = 64
 CY = 8
+
+
+def add_all(block, axis):
+    parts = lax.all_gather(block, axis)
+    return jnp.sum(parts, axis=0)
 
 
 def extended(cells, sides, width):
@@ -80,9 +85,7 @@
             )
     conv_out = result.astype(jnp.bfloat16).reshape(chans, rows_x, CY * NZ)
     total_cells = rows_x * n_region * CY * n_narrow * NZ
-    weight_grad = lax.psum(jnp.stack(kernels), ("narrow", "region")) * (
-        1.0 / math.sqrt(total_cells)
-    )
+    weight_grad = add_all(jnp.stack(kernels), ("narrow", "region")) * (1.0 / math.sqrt(total_cells))
     grad_flat = backward.astype(jnp.bfloat16).reshape(chans, voxels)
     picked = jnp.take(grad_flat, targets, axis=1).T.reshape(devices, slots * chans)
     returned = lax.all_to_all(picked, ("narrow", "region"), split_axis=0, concat_axis=0, tiled=True)

time: 696 us -> 568 us (0.82)
  waiting for transfers between devices: 126 us -> 26.8 us
  local copies, waits for them, and re-layouts: 201 us -> 134 us
  blocking collectives: 0 us -> 40.5 us
  starting transfers between devices: 58.1 us -> 49.9 us
    psum x1 -> x0, waiting for transfers between devices: 114 us -> none  [shards(): lax.psum(jnp.stack(kernels), ('narrow', 'region'))]
    gather x1, local copies, waits for them, and re-layouts: 67.6 us -> 22 us  [shards(): point_grad = returned[owner, slot].T]
    all_to_all x0 -> x1, blocking collectives: none -> 40.5 us  [shards(): lax.all_to_all(picked, ('narrow', 'region'), split_axis=0, concat_axis=0,...]
    all_to_all x1 -> x0, starting transfers between devices: 21.9 us -> none  [shards(): lax.all_to_all(picked, ('narrow', 'region'), split_axis=0, concat_axis=0,...]
    ppermute x4, starting transfers between devices: 5.16 us -> 18 us  [extended(): lax.ppermute(head, axis, [((i + 1) % count, i) for i in range(ends)])]
    unnamed x46 -> x52, local copies, waits for them, and re-layouts: 57.5 us -> 46.1 us
    all_to_all x1, waiting for transfers between devices: 0.01 us -> 11.3 us  [shards(): lax.all_to_all(send_feats, ('narrow', 'region'), split_axis=0, concat_axi...]
    reduce_sum x0 -> x1, other arithmetic: none -> 8.19 us  [add_all(): return jnp.sum(parts, axis=0)]
  transfers between devices with their start and end apart: 12 -> 11, of which waited for: 4 -> 5; matrix products, arithmetic and copies ran while one was open for 53% -> 49% of each run, Pallas kernels for 0% -> 0%
where the time goes in v1:
time: 568 us; the launch traced here: 558 us
  other arithmetic  161 us (28%)
  local copies, waits for them, and re-layouts  134 us (24%)
  matrix products  131 us (23%)
  starting transfers between devices  49.9 us (9%)
  blocking collectives  40.5 us (7%)
  waiting for transfers between devices  26.8 us (5%)
  between operations  15 us (3%)
    dot_general x9, matrix products, shards(): jnp.einsum('ok,kxyz->oxyz', weight[k], window, preferred_element_type=jnp...  59.6 us
    dot_general x9, matrix products, shards(): jnp.einsum('ck,kxyz->cxyz', flipped[k], gstack[:, 2 - a:2 - a + rows_x, 2...  52.4 us
    scatter-add x1, other arithmetic, shards(): sums = jax.ops.segment_sum(incoming, targets, num_segments=voxels)  52.4 us
    unnamed x52, local copies, waits for them, and re-layouts  46.1 us
    all_to_all x1, blocking collectives, shards(): lax.all_to_all(picked, ('narrow', 'region'), split_axis=0, concat_axis=0,...  40.5 us
    gather x1, local copies, waits for them, and re-layouts, shards(): jnp.take(grad_flat, targets, axis=1).T.reshape(devices, slots * chans)  29.4 us
    concatenate x2, other arithmetic, stack_depth(): return jnp.concatenate([padded[..., o:o + depth] for o in offsets], axis=0)  22.5 us
    gather x1, local copies, waits for them, and re-layouts, shards(): point_grad = returned[owner, slot].T  22 us
  transfers between devices with their start and end apart: 11, of which 5 were waited for; matrix products, arithmetic and copies ran while one was open for 49% of the time, Pallas kernels for 0%

profile of v1, /device:TPU:0, one launch (start us, length us, event | category | flops | bytes accessed | tf_op | source)
XLA Modules:
  0.0 558.0 jit_solution(3888486853055913269)
XLA Ops:
  7.9 9.2 %reduce-window.6 = s32[32,32,128]{2,1,0:T(8,128)S(1)} reduce-window(s32[32,32,128]{2,1,0:T(8,128)S(1)} %fusion.21, s32[]{:T(128)} %constant.14.clone.1), window={size=1x1x128 pad=0_0x0_0x127_0}, to_apply=%region_0.0 | reduce-window | flops 16646144 | bytes 1048580 | tf_op jit(solution)/shard_map/reduce-window
  23.9 11.6 %scatter_custom_fusion.2 = bf16[8192,64]{1,0:T(8,128)(2,1)S(1)} fusion(s32[4096]{0:T(1024)S(1)} %broadcast_select_fusion.1, bf16[4096,64]{1,0:T(8,128)(2,1)S(1)} %copy.54, bf16[]{:T(256)} %constant.34.clone.1), kind=kCustom, calls=%fused_computation.45 | custom fusion | bytes 1048578
  39.7 8.4 %reduce.11 = bf16[32,16384]{1,0:T(8,128)(2,1)S(1)} reduce(bf16[32,1,16384]{2,1,0:T(2,128)(2,1)} %all_to_all.24, bf16[]{:T(256)} %broadcast.231), dimensions={1}, to_apply=%all_to_all.24.reduce_sub_computation | reduce | bytes 2097154 | tf_op jit(solution)/shard_map/all_to_all | solution.py:52
  49.7 7.6 %all-to-all-start.1 = ((bf16[32,2,8192]{2,1,0:T(2,128)(2,1)}), bf16[32,2,8192]{2,1,0:T(2,128)(2,1)S(1)}, u32[]{:S(2)}, u32[]{:S(2)}) async-start(bf16[32,2,8192]{2,1,0:T(2,128)(2,1)} %reshape.225), calls=%async_computation.1 | async-start | bytes 2097152 | tf_op jit(solution)/shard_map/all_to_all | solution.py:52
  57.3 16.3 %scatter_custom_fusion.1 = s32[8192]{0:T(1024)} fusion(s32[4096]{0:T(1024)S(1)} %broadcast_select_fusion.1, s32[4096]{0:T(1024)} %param.7, s32[]{:T(128)} %constant.14.clone.1), kind=kCustom, calls=%fused_computation.98 | custom fusion | bytes 33280
  73.6 11.3 %all-to-all-done.1 = bf16[32,2,8192]{2,1,0:T(2,128)(2,1)S(1)} async-done(((bf16[32,2,8192]{2,1,0:T(2,128)(2,1)}), bf16[32,2,8192]{2,1,0:T(2,128)(2,1)S(1)}, u32[]{:S(2)}, u32[]{:S(2)}) %all-to-all-start.1) | async-done | bytes 1048608 | tf_op jit(solution)/shard_map/all_to_all | solution.py:52
  90.9 7.7 %convert_reduce_fusion = f32[32,16384]{1,0:T(8,128)S(1)} fusion(bf16[32,1,16384]{2,1,0:T(2,128)(2,1)} %reshape.226), kind=kLoop, calls=%fused_computation.25 | loop fusion | flops 524288 | bytes 3145728 | tf_op jit(solution)/shard_map/convert_element_type | solution.py:55
  101.7 52.4 %scatter_custom_fusion = f32[12288,64]{1,0:T(8,128)} fusion(s32[8192]{0:T(1024)S(1)} %bitcast.291, f32[8192,64]{1,0:T(8,128)} %reshape.171, f32[]{:T(128)} %constant.13.clone.1), kind=kCustom, calls=%fused_computation.23 | custom fusion | flops 524288 | bytes 3146240 | tf_op jit(solution)/shard_map/scatter-add | solution.py:57
  157.2 8.3 %collective-permute-start = (bf16[64,24,1,64]{0,3,2,1:T(8,128)(2,1)S(1)}, bf16[64,24,1,64]{0,3,2,1:T(8,128)(2,1)S(1)}, u32[]{:S(2)}, u32[]{:S(2)}) collective-permute-start(bf16[64,24,1,64]{0,3,2,1:T(8,128)(2,1)S(1)} %get-tuple-element.24), channel_id=1, source_target_pairs={{0,8},{8,16},{16,24},{1,9},{9,17},{17,25},{2,10},{10,18},{18,26},{... | collective-permute-start | bytes 589832 | tf_op jit(solution)/shard_map/ppermute | solution.py:24
  179.4 14.1 %collective-permute-start.3 = (bf16[64,1,10,64]{0,3,2,1:T(8,128)(2,1)}, bf16[64,1,10,64]{0,3,2,1:T(8,128)(2,1)}, u32[]{:S(2)}, u32[]{:S(2)}) collective-permute-start(bf16[64,1,10,64]{0,3,2,1:T(8,128)(2,1)} %get-tuple-element.21), channel_id=1, source_target_pairs={{1,0},{2,1},{3,2},{4,3},{5,4},{6,5},{7,6},{9,8},{10,9},{11,10},{12... | collective-permute-start | bytes 245768 | tf_op jit(solution)/shard_map/ppermute | solution.py:26
  197.0 9.6 %select_maximum_fusion.4 = bf16[64,26,10,66]{0,3,2,1:T(8,128)(2,1)S(1)} fusion(bf16[64,1,10,64]{0,3,2,1:T(8,128)(2,1)} %collective-permute-done.3, bf16[64,1,10,64]{0,3,2,1:T(8,128)(2,1)} %collective-permute-done.2, bf16[64,24,1,64]{0,3,2,1:T(8,128)(2,1)} %copy-done.4, bf16[64,24,8,64]{0,3,2,1:T(8,128)(2,1)} %bitcast.282, ...), kind=kLoop, calls=%fused_computation.16 | loop fusion | flops 19768320 | bytes 4326400 | tf_op jit(solution)/shard_map/concatenate | solution.py:22
  209.0 11.1 %pad_maximum_fusion = bf16[192,26,10,64]{0,3,2,1:T(8,128)(2,1)S(1)} fusion(bf16[64,26,10,64]{0,3,2,1:T(8,128)(2,1)S(1)} %get-tuple-element.17, bf16[64,1,10,64]{0,3,2,1:T(8,128)(2,1)} %collective-permute-done.3, bf16[64,24,1,64]{0,3,2,1:T(8,128)(2,1)S(1)} %copy-done.5, bf16[64,24,8,64]{0,3,2,1:T(8,128)(2,1)S(1)} %bitcast.283, ...), kind=kLoop, calls=%fused_computation.8 | loop fusion | flops 44728320 | bytes 12779520 | tf_op jit(solution)/shard_map/concatenate | solution.py:34
  240.0 9.1 %collective-permute-start.4 = (bf16[64,24,1,64]{0,3,2,1:T(8,128)(2,1)}, bf16[64,24,1,64]{0,3,2,1:T(8,128)(2,1)S(1)}, u32[]{:S(2)}, u32[]{:S(2)}) collective-permute-start(bf16[64,24,1,64]{0,3,2,1:T(8,128)(2,1)} %get-tuple-element.22), channel_id=1, source_target_pairs={{0,8},{8,16},{16,24},{1,9},{9,17},{17,25},{2,10},{10,18},{18,26},{... | collective-permute-start | bytes 589832 | tf_op jit(solution)/shard_map/ppermute | solution.py:24
  279.9 9.4 %select_maximum_fusion = bf16[64,26,10,66]{0,3,2,1:T(8,128)(2,1)S(1)} fusion(bf16[64,1,10,64]{0,3,2,1:T(8,128)(2,1)S(1)} %collective-permute-done.7, bf16[64,1,10,64]{0,3,2,1:T(8,128)(2,1)S(1)} %collective-permute-done.6, bf16[64,24,1,64]{0,3,2,1:T(8,128)(2,1)} %collective-permute-done.5, bf16[64,24,8,64]{0,3,2,1:T(8,128)(2,1)S(1)} %bitcast.277, ...), kind=kLoop, calls=%fused_computation.12 | loop fusion | flops 19768320 | bytes 4326400 | tf_op jit(solution)/shard_map/concatenate | solution.py:22
  291.6 11.4 %pad_maximum_fusion.1 = bf16[192,26,10,64]{0,3,2,1:T(8,128)(2,1)S(1)} fusion(bf16[64,26,10,64]{0,3,2,1:T(8,128)(2,1)S(1)} %get-tuple-element.15, bf16[64,1,10,64]{0,3,2,1:T(8,128)(2,1)S(1)} %collective-permute-done.7, bf16[64,24,1,64]{0,3,2,1:T(8,128)(2,1)} %collective-permute-done.5, bf16[64,24,8,64]{0,3,2,1:T(8,128)(2,1)S(1)} %bitcast.278, ...), kind=kLoop, calls=%fused_computation.9 | loop fusion | flops 44728320 | bytes 12779520 | tf_op jit(solution)/shard_map/concatenate | solution.py:34
  338.5 17.0 %add_convert_fusion = bf16[24,8,64,64]{3,2,1,0:T(8,128)(2,1)S(1)} fusion(f32[24,8,64,64]{3,2,1,0:T(8,128)} %fusion.62, f32[24,8,64,64]{3,2,1,0:T(8,128)} %fusion.61, f32[24,8,64,64]{3,2,1,0:T(8,128)} %fusion.60, f32[24,8,64,64]{3,2,1,0:T(8,128)} %fusion.59, f32[24,8,64,64]{3,2,1,0:T(8,128)} %fusion.58, f32[24,8,64,64]{3,2,1,0:T(8,128)} %fusion.57, ...), kind=kOutput, calls=%fused_computation.10 | convolution fusion | flops 309067776 | bytes 33153024 | tf_op jit(solution)/shard_map/ck,kxyz->cxyz/dot_general | solution.py:80
  355.5 29.4 %gather_fusion = bf16[8192,64]{1,0:T(8,128)(2,1)} fusion(bf16[64,12288]{0,1:T(8,128)(2,1)S(1)} %bitcast.284, s32[8192]{0:T(1024)S(1)} %copy-done.17), kind=kCustom, calls=%fused_computation | custom fusion | bytes 2129920 | tf_op jit(solution)/shard_map/jit(_take)/gather | solution.py:90
  394.4 8.4 %reduce.12 = bf16[32,16384]{1,0:T(8,128)(2,1)S(1)} reduce(bf16[32,1,16384]{2,1,0:T(2,128)(2,1)} %all_to_all.25, bf16[]{:T(256)} %broadcast.231), dimensions={1}, to_apply=%all_to_all.25.reduce_sub_computation | reduce | bytes 2097154 | tf_op jit(solution)/shard_map/all_to_all | solution.py:91
  403.7 40.5 %all_to_all.29 = bf16[32,2,8192]{2,1,0:T(2,128)(2,1)S(1)} all-to-all(bf16[32,2,8192]{2,1,0:T(2,128)(2,1)S(1)} %reshape.227), channel_id=1, replica_groups=mesh['narrow'=4,'region'=8] {'narrow','region'}, dimensions={0} | all-to-all | bytes 2097152 | tf_op jit(solution)/shard_map/all_to_all | solution.py:91
  454.0 22.0 %gather_fusion.1 = bf16[4096,64]{1,0:T(8,128)(2,1)S(1)} fusion(bf16[32,256,64]{2,1,0:T(8,128)(2,1)S(1)} %reshape.141, s32[4096]{0:T(1024)S(1)} %bitcast.279), kind=kCustom, calls=%fused_computation.1 | custom fusion | bytes 1081344 | tf_op jit(solution)/shard_map/gather | solution.py:93
  477.1 7.3 %fusion.23 = f32[24,8,64,64]{3,2,1,0:T(8,128)} fusion(bf16[192,26,10,64]{0,3,2,1:T(8,128)(2,1)} %copy-done, bf16[9,64,192]{2,1,0:T(8,128)(2,1)S(1)} %copy-done.6), kind=kOutput, calls=%fused_computation.69 | convolution fusion | flops 301989888 | bytes 9568256 | tf_op jit(solution)/shard_map/ok,kxyz->oxyz/dot_general | solution.py:74
  484.4 7.2 %fusion.25 = f32[24,8,64,64]{3,2,1,0:T(8,128)} fusion(bf16[192,26,10,64]{0,3,2,1:T(8,128)(2,1)} %copy-done, bf16[9,64,192]{2,1,0:T(8,128)(2,1)S(1)} %copy-done.6), kind=kOutput, calls=%fused_computation.71 | convolution fusion | flops 301989888 | bytes 9568256 | tf_op jit(solution)/shard_map/ok,kxyz->oxyz/dot_general | solution.py:74
  518.1 18.7 %add_convert_fusion.1 = bf16[24,8,64,64]{3,2,1,0:T(8,128)(2,1)} fusion(f32[24,8,64,64]{3,2,1,0:T(8,128)} %fusion.23, f32[24,8,64,64]{3,2,1,0:T(8,128)} %fusion.25, f32[24,8,64,64]{3,2,1,0:T(8,128)} %fusion.27, f32[24,8,64,64]{3,2,1,0:T(8,128)} %fusion.29, f32[24,8,64,64]{3,2,1,0:T(8,128)} %fusion.31, f32[24,8,64,64]{3,2,1,0:T(8,128)} %fusion.33, ...), kind=kOutput, calls=%fused_computation.11 | convolution fusion | flops 309067776 | bytes 35291136 | tf_op jit(solution)/shard_map/ok,kxyz->oxyz/dot_general | solution.py:74
  541.6 8.2 %reduce_sum.19 = f32[9,64,192]{2,1,0:T(8,128)S(1)} reduce(f32[32,9,64,192]{3,2,1,0:T(8,128)} %bitcast.285, f32[]{:T(128)} %constant.13.clone.1), dimensions={0}, to_apply=%region_6.7 | reduce | flops 3428352 | bytes 14598148 | tf_op jit(solution)/shard_map/reduce_sum | solution.py:13
  (131 shorter events, 187.0 us)
Async XLA Ops:
  49.7 35.1 %all-to-all-start.1 = ((bf16[32,2,8192]{2,1,0:T(2,128)(2,1)}), bf16[32,2,8192]{2,1,0:T(2,128)(2,1)S(1)}, u32[]{:S(2)}, u32[]{:S(2)}) async-start(bf16[32,2,8192]{2,1,0:T(2,128)(2,1)} %reshape.225), calls=%async_computation.1 | async-start | bytes 2097152 | tf_op jit(solution)/shard_map/all_to_all | solution.py:52
  84.9 16.9 %all-to-all-start = ((s32[32,1,256]{2,1,0:T(1,128)}), s32[32,1,256]{2,1,0:T(1,128)S(1)}, u32[]{:S(2)}, u32[]{:S(2)}) async-start(s32[32,1,256]{2,1,0:T(1,128)} %bitcast.5), calls=%async_computation | async-start | bytes 65536 | tf_op jit(solution)/shard_map/all_to_all | solution.py:53
  87.4 454.2 %all-gather.3.cloned.1.call-start = ((), (), s32[]{:S(2)}) async-start(), calls=%async_computation.3 | async-start | bytes 19464192 | tf_op jit(solution)/shard_map/all_gather | solution.py:12
  101.7 55.4 %copy-start.7 = (s32[32,1,256]{2,1,0:T(1,128)}, s32[32,1,256]{2,1,0:T(1,128)S(1)}, u32[]{:S(2)}) copy-start(s32[32,1,256]{2,1,0:T(1,128)S(1)} %all-to-all-done) | copy-start | bytes 98308
  157.1 22.3 %copy-start.2 = (bf16[12288,64]{1,0:T(8,128)(2,1)}, bf16[12288,64]{1,0:T(8,128)(2,1)S(1)}, u32[]{:S(2)}) copy-start(bf16[12288,64]{1,0:T(8,128)(2,1)S(1)} %convert_element_type.29) | copy-start | bytes 4718596
  157.2 13.5 %collective-permute-start = (bf16[64,24,1,64]{0,3,2,1:T(8,128)(2,1)S(1)}, bf16[64,24,1,64]{0,3,2,1:T(8,128)(2,1)S(1)}, u32[]{:S(2)}, u32[]{:S(2)}) collective-permute-start(bf16[64,24,1,64]{0,3,2,1:T(8,128)(2,1)S(1)} %get-tuple-element.24), channel_id=1, source_target_pairs={{0,8},{8,16},{16,24},{1,9},{9,17},{17,25},{2,10},{10,18},{18,26},{... | collective-permute-start | bytes 589832 | tf_op jit(solution)/shard_map/ppermute | solution.py:24
  165.4 11.2 %collective-permute-start.1 = (bf16[64,24,1,64]{0,3,2,1:T(8,128)(2,1)S(1)}, bf16[64,24,1,64]{0,3,2,1:T(8,128)(2,1)S(1)}, u32[]{:S(2)}, u32[]{:S(2)}) collective-permute-start(bf16[64,24,1,64]{0,3,2,1:T(8,128)(2,1)S(1)} %get-tuple-element.25), channel_id=1, source_target_pairs={{8,0},{16,8},{24,16},{9,1},{17,9},{25,17},{10,2},{18,10},{26,18},{... | collective-permute-start | bytes 589832 | tf_op jit(solution)/shard_map/ppermute | solution.py:26
  177.5 19.5 %collective-permute-start.2 = (bf16[64,1,10,64]{0,3,2,1:T(8,128)(2,1)}, bf16[64,1,10,64]{0,3,2,1:T(8,128)(2,1)}, u32[]{:S(2)}, u32[]{:S(2)}) collective-permute-start(bf16[64,1,10,64]{0,3,2,1:T(8,128)(2,1)} %get-tuple-element.20), channel_id=1, source_target_pairs={{0,1},{1,2},{2,3},{3,4},{4,5},{5,6},{6,7},{8,9},{9,10},{10,11},{11... | collective-permute-start | bytes 245768 | tf_op jit(solution)/shard_map/ppermute | solution.py:24
  179.4 17.6 %collective-permute-start.3 = (bf16[64,1,10,64]{0,3,2,1:T(8,128)(2,1)}, bf16[64,1,10,64]{0,3,2,1:T(8,128)(2,1)}, u32[]{:S(2)}, u32[]{:S(2)}) collective-permute-start(bf16[64,1,10,64]{0,3,2,1:T(8,128)(2,1)} %get-tuple-element.21), channel_id=1, source_target_pairs={{1,0},{2,1},{3,2},{4,3},{5,4},{6,5},{7,6},{9,8},{10,9},{11,10},{12... | collective-permute-start | bytes 245768 | tf_op jit(solution)/shard_map/ppermute | solution.py:26
  220.0 17.0 %copy-start = (bf16[192,26,10,64]{0,3,2,1:T(8,128)(2,1)}, bf16[192,26,10,64]{0,3,2,1:T(8,128)(2,1)S(1)}, u32[]{:S(2)}) copy-start(bf16[192,26,10,64]{0,3,2,1:T(8,128)(2,1)S(1)} %pad_maximum_fusion) | copy-start | bytes 19169284
  240.0 29.0 %collective-permute-start.4 = (bf16[64,24,1,64]{0,3,2,1:T(8,128)(2,1)}, bf16[64,24,1,64]{0,3,2,1:T(8,128)(2,1)S(1)}, u32[]{:S(2)}, u32[]{:S(2)}) collective-permute-start(bf16[64,24,1,64]{0,3,2,1:T(8,128)(2,1)} %get-tuple-element.22), channel_id=1, source_target_pairs={{0,8},{8,16},{16,24},{1,9},{9,17},{17,25},{2,10},{10,18},{18,26},{... | collective-permute-start | bytes 589832 | tf_op jit(solution)/shard_map/ppermute | solution.py:24
  249.1 22.5 %collective-permute-start.5 = (bf16[64,24,1,64]{0,3,2,1:T(8,128)(2,1)}, bf16[64,24,1,64]{0,3,2,1:T(8,128)(2,1)}, u32[]{:S(2)}, u32[]{:S(2)}) collective-permute-start(bf16[64,24,1,64]{0,3,2,1:T(8,128)(2,1)} %get-tuple-element.23), channel_id=1, source_target_pairs={{8,0},{16,8},{24,16},{9,1},{17,9},{25,17},{10,2},{18,10},{26,18},{... | collective-permute-start | bytes 589832 | tf_op jit(solution)/shard_map/ppermute | solution.py:26
  272.5 4.5 collective-permute-start.6
  274.9 5.0 collective-permute-start.7
  291.6 11.4 %copy-start.9 = (bf16[1,64,3,64]{1,3,2,0:T(8,128)(2,1)S(1)}, bf16[1,64,3,64]{1,3,2,0:T(8,128)(2,1)}, u32[]{:S(2)}) copy-start(bf16[1,64,3,64]{1,3,2,0:T(8,128)(2,1)} %copy.58) | copy-start | bytes 73732
  325.0 4.5 copy-start.15
  329.5 4.4 copy-start.16
  334.0 4.5 copy-start.8
  338.5 17.0 %copy-start.17 = (s32[8192]{0:T(1024)S(1)}, s32[8192]{0:T(1024)}, u32[]{:S(2)}) copy-start(s32[8192]{0:T(1024)} %broadcast_clamp_fusion) | copy-start | bytes 98308
  403.7 50.3 %copy-start.1 = (s32[4096,1]{0,1:T(1,128)S(1)}, s32[4096,1]{0,1:T(1,128)}, u32[]{:S(2)}) copy-start(s32[4096,1]{0,1:T(1,128)} %get-tuple-element.12) | copy-start | bytes 49156
  454.0 23.1 %copy-start.6 = (bf16[9,64,192]{2,1,0:T(8,128)(2,1)S(1)}, bf16[9,64,192]{2,1,0:T(8,128)(2,1)}, u32[]{:S(2)}) copy-start(bf16[9,64,192]{2,1,0:T(8,128)(2,1)} %param.8) | copy-start | bytes 663556
  477.1 14.6 %slice-start = ((s8[8519680]{0:T(1024)(128)(4,1)}), s8[4194304]{0:T(1024)(128)(4,1)S(1)}, s32[]{:S(2)}) async-start(s8[8519680]{0:T(1024)(128)(4,1)} %bitcast.264), calls=%async_computation.4 | async-start | bytes 8388608
  477.1 14.6 %slice-start.1 = ((s8[8519680]{0:T(1024)(128)(4,1)}), s8[4194304]{0:T(1024)(128)(4,1)S(1)}, s32[]{:S(2)}) async-start(s8[8519680]{0:T(1024)(128)(4,1)} %bitcast.264), calls=%async_computation.5 | async-start | bytes 8388608
  484.4 7.2 %slice-start.2 = ((s8[8519680]{0:T(1024)(128)(4,1)}), s8[131072]{0:T(1024)(128)(4,1)S(1)}, s32[]{:S(2)}) async-start(s8[8519680]{0:T(1024)(128)(4,1)} %bitcast.264), calls=%async_computation.6 | async-start | bytes 262144
  (8 other events, 29.5 us)
Sparse Core Ops, SparseCore 0:
  239.2 136.3 all-gather.2
